TPU v7x, 512 devices: a whole 4x8x8 slice. The times are simulated.
512 devices in a mesh: ctx: 64 (over z, y), mp: 8 (over x, core).
Axes of the slice: x: 4, y: 8, z: 8, core: 2. Of those that a mesh axis runs over, the one named last changes fastest.
Arguments:
- seq_in: bfloat16 [8192, 8192], P('ctx', 'mp'), may hold values from -6 to 6
- gate_in: bfloat16 [8192, 8192], P('ctx', 'mp'), may hold values from -6 to 6
- upstream: bfloat16 [8192, 8192], P('ctx', 'mp'), may hold values from -6 to 6
- forget_flags: int32 [8192], P('ctx'), may hold values 0 or 1
- conv_weight: float32 [4, 8192], P(None, 'mp'), may hold values from -3 to 3
- conv_bias: float32 [8192], P('mp'), may hold values from -3 to 3
- proj_weight: bfloat16 [8192, 544], P(('mp', 'ctx')), may hold values from -0.0625 to 0.0625
- dt_weight: bfloat16 [512, 8192], P('ctx', 'mp'), may hold values from -0.25 to 0.25
- dt_bias: float32 [8192], P('mp'), may hold values from -10 to -3
- a_log: float32 [16, 8192], P(None, 'mp'), may hold values from 0 to 2.77
- skip_gain: float32 [8192], P('mp'), may hold values from 0.5 to 1.5
Outputs:
- grad_seq: bfloat16 [8192, 8192], P('ctx', 'mp')
- grad_gate: bfloat16 [8192, 8192], P('ctx', 'mp')
- grad_dt_weight: float32 [512, 8192], P('ctx', 'mp')
- grad_conv_weight: float32 [4, 8192], P(None, ('mp', 'ctx'))
- grad_conv_bias: float32 [8192], P(('mp', 'ctx'))
- grad_dt_bias: float32 [8192], P(('mp', 'ctx'))
- grad_a_log: float32 [16, 8192], P(None, ('mp', 'ctx'))
- grad_skip: float32 [8192], P(('mp', 'ctx'))
All inputs are finite; a program needn't handle non-finite values. No bound on the sum of `forget_flags` on one device may be relied on, other than what follows from the above.
Results may differ from a plain program's by a relative error of at most 0.017.
Values may be sent and summed in bfloat16 or wider, within the bound.
A program may use at most 64 MiB of HBM per device.

v0:
```python
import jax
import jax.numpy as jnp
from jax import lax
from jax.sharding import PartitionSpec as P

STATE = 16
RANK = 512
CONV = 4


def shifted(block, axis, distance):
    devices = range(lax.axis_size(axis))
    route = [(i - distance, i) for i in devices if i - distance in devices]
    return lax.ppermute(block, axis, route)


def prefix(x, axis, combine, identity, reverse):
    count, mine = (lax.axis_size(axis), lax.axis_index(axis))
    everything = jax.tree.map(lambda part: lax.all_gather(part, axis), x)
    start = jax.tree.map(
        lambda part, zero: jnp.broadcast_to(jnp.asarray(zero, part.dtype), part.shape), x, identity
    )

    def step(k, before):
        at = count - 1 - k if reverse else k
        reached = at > mine if reverse else at < mine
        new = combine(before, jax.tree.map(lambda part: part[at], everything))
        return jax.tree.map(lambda a, b: jnp.where(reached, a, b), new, before)

    return lax.fori_loop(0, count, step, start)


def to_blocks(arrays):
    return tuple((a.reshape((a.shape[0] // 16, 16) + a.shape[1:]) for a in arrays))


def block_closed(carry, inputs):
    state, a_matrix = carry
    act_blk, step_blk, b_blk, c_blk = inputs
    rows = step_blk.shape[0]
    cumul = jnp.cumsum(step_blk[:, None, :] * a_matrix[None], axis=0)
    later_rows = lax.broadcasted_iota(jnp.int32, (rows, rows), 0)
    early_rows = lax.broadcasted_iota(jnp.int32, (rows, rows), 1)
    lower = (later_rows >= early_rows)[:, :, None, None]
    gaps = jnp.where(lower, cumul[:, None] - cumul[None, :], 0.0)
    weights = jnp.where(lower, jnp.exp(gaps), 0.0)
    inflow = b_blk[:, :, None] * (step_blk * act_blk)[:, None, :]
    states = jnp.exp(cumul) * state[None] + jnp.sum(weights * inflow[None], axis=1)
    outputs = jnp.sum(c_blk[:, :, None] * states, axis=1)
    return ((states[-1], a_matrix), outputs)


def scan_tokens(act_full, step_size, b_matrix, c_matrix, log_rates, skip):
    a_matrix = -jnp.exp(log_rates)
    length = act_full.shape[0]
    start_state = jnp.zeros(log_rates.shape, jnp.float32)
    carry, outputs = lax.scan(
        jax.checkpoint(block_closed),
        (start_state, a_matrix),
        to_blocks((act_full, step_size, b_matrix, c_matrix)),
    )
    return (outputs.reshape(length, -1) + skip[None, :] * act_full, carry[0])


def carry_block(carry, inputs):
    state, a_matrix = carry
    step_blk, c_blk = inputs
    cumul = jnp.cumsum(step_blk[:, None, :] * a_matrix[None], axis=0)
    states = jnp.exp(cumul) * state[None]
    return ((states[-1], a_matrix), jnp.sum(c_blk[:, :, None] * states, axis=1))


def carry_in(step_size, c_matrix, log_rates, state_in):
    a_matrix = -jnp.exp(log_rates)
    length = step_size.shape[0]
    carry, outputs = lax.scan(
        jax.checkpoint(carry_block), (state_in, a_matrix), to_blocks((step_size, c_matrix))
    )
    return (outputs.reshape(length, -1), carry[0])


def compose(earlier, later):
    return (earlier[0] * later[0], later[0] * earlier[1] + later[1])


def body(
    seq_in,
    gate_in,
    upstream,
    forget_flags,
    conv_weight,
    conv_bias,
    proj_weight,
    dt_weight,
    dt_bias,
    a_log,
    skip_gain,
):
    length = seq_in.shape[0]
    rim_rows = CONV - 1
    from_left = shifted(seq_in[length - rim_rows :], "ctx", 1)
    padded = jnp.concatenate([from_left, seq_in], axis=0)
    pre_act = jnp.zeros(seq_in.shape, jnp.float32) + conv_bias[None, :]
    for k in range(CONV):
        pre_act = pre_act + conv_weight[k][None, :] * padded[k : k + length]
    act_half = jax.nn.silu(pre_act).astype(jnp.bfloat16)
    rows_proj, rows_dt = (
        lax.all_gather(proj_weight, "ctx", axis=0, tiled=True),
        lax.all_gather(dt_weight, "ctx", axis=0, tiled=True),
    )
    partial_proj = jnp.dot(act_half, rows_proj, preferred_element_type=jnp.float32)
    projected = lax.psum(partial_proj, "mp")
    dt_low = projected[:, :RANK].astype(jnp.bfloat16)
    b_matrix = projected[:, RANK : RANK + STATE]
    c_matrix = projected[:, RANK + STATE :]
    dt_pre = jnp.dot(dt_low, rows_dt, preferred_element_type=jnp.float32) + dt_bias[None, :]
    step_size = jax.nn.softplus(dt_pre)
    a_matrix = -jnp.exp(a_log)
    act_full = act_half.astype(jnp.float32)
    (mixed_local, state_end), pull_local = jax.vjp(
        scan_tokens, act_full, step_size, b_matrix, c_matrix, a_log, skip_gain
    )
    zeros_state = jnp.zeros_like(state_end)
    step_totals = jnp.sum(step_size, axis=0)
    decays = jnp.exp(a_matrix * step_totals[None, :])
    state_in = prefix(
        (decays, state_end), "ctx", compose, (jnp.ones_like(decays), zeros_state), False
    )[1]
    (mixed_carry, unused_end), pull_carry = jax.vjp(carry_in, step_size, c_matrix, a_log, state_in)
    mixed = mixed_local + mixed_carry
    flag_values = forget_flags.astype(jnp.float32)
    grad_out = -flag_values[:, None] * upstream.astype(jnp.float32)
    gate_full = gate_in.astype(jnp.float32)
    gate_sigmoid = jax.nn.sigmoid(gate_full)
    grad_mixed = grad_out * (gate_full * gate_sigmoid)
    grad_gate = (
        grad_out * mixed * (gate_sigmoid * (1.0 + gate_full * (1.0 - gate_sigmoid)))
    ).astype(jnp.bfloat16)
    local_adjoint = pull_carry((grad_mixed, zeros_state))[3]
    adjoint_out = prefix(
        (decays, local_adjoint), "ctx", compose, (jnp.ones_like(decays), zeros_state), True
    )[1]
    grad_act_scan, grad_step, grad_bmat, grad_cmat, grad_rate, grad_skip = pull_local(
        (grad_mixed, adjoint_out)
    )
    extra_step, extra_cmat, extra_rate, unused_in = pull_carry((grad_mixed, adjoint_out))
    grad_step = grad_step + extra_step
    grad_cmat = grad_cmat + extra_cmat
    grad_rate = grad_rate + extra_rate
    grad_pre = grad_step * jax.nn.sigmoid(dt_pre)
    grad_pre_half = grad_pre.astype(jnp.bfloat16)
    grad_dtw = lax.dot_general(
        dt_low, grad_pre_half, (((0,), (0,)), ((), ())), preferred_element_type=jnp.float32
    )
    grad_low = lax.dot_general(
        grad_pre_half, rows_dt, (((1,), (1,)), ((), ())), preferred_element_type=jnp.float32
    )
    grad_proj = lax.psum(
        jnp.concatenate([grad_low, grad_bmat, grad_cmat], axis=1).astype(jnp.bfloat16), "mp"
    )
    grad_from_proj = lax.dot_general(
        grad_proj, rows_proj, (((1,), (1,)), ((), ())), preferred_element_type=jnp.float32
    )
    act_sigmoid = jax.nn.sigmoid(pre_act)
    grad_pre_act = (grad_act_scan + grad_from_proj) * (
        act_sigmoid * (1.0 + pre_act * (1.0 - act_sigmoid))
    )
    from_next = shifted(grad_pre_act[:rim_rows], "ctx", -1)
    grad_padded = jnp.concatenate([grad_pre_act, from_next], axis=0)
    grad_seq = jnp.zeros(seq_in.shape, jnp.float32)
    for k in range(CONV):
        grad_seq = (
            grad_seq + conv_weight[k][None, :] * grad_padded[rim_rows - k : rim_rows - k + length]
        )
    grad_conv_w = jnp.stack(
        [jnp.sum(grad_pre_act * padded[k : k + length], axis=0) for k in range(CONV)]
    )
    grad_conv_b = jnp.sum(grad_pre_act, axis=0)
    grad_dt_b = jnp.sum(grad_pre, axis=0)
    summed_grads = (
        lax.psum_scatter(grad_dtw, "ctx", scatter_dimension=0, tiled=True),
        lax.psum_scatter(grad_conv_w, "ctx", scatter_dimension=1, tiled=True),
        lax.psum_scatter(grad_conv_b, "ctx", scatter_dimension=0, tiled=True),
        lax.psum_scatter(grad_dt_b, "ctx", scatter_dimension=0, tiled=True),
        lax.psum_scatter(grad_rate, "ctx", scatter_dimension=1, tiled=True),
        lax.psum_scatter(grad_skip, "ctx", scatter_dimension=0, tiled=True),
    )
    return (grad_seq.astype(jnp.bfloat16), grad_gate) + tuple(summed_grads)


def solution(mesh):
    return jax.shard_map(
        body,
        mesh=mesh,
        in_specs=(
            P("ctx", "mp"),
            P("ctx", "mp"),
            P("ctx", "mp"),
            P("ctx"),
            P(None, "mp"),
            P("mp"),
            P(("mp", "ctx"), None),
            P("ctx", "mp"),
            P("mp"),
            P(None, "mp"),
            P("mp"),
        ),
        out_specs=(
            P("ctx", "mp"),
            P("ctx", "mp"),
            P("ctx", "mp"),
            P(None, ("mp", "ctx")),
            P(("mp", "ctx")),
            P(("mp", "ctx")),
            P(None, ("mp", "ctx")),
            P(("mp", "ctx")),
        ),
        check_vma=False,
    )
```

profile of v0, /device:TPU:6, one launch (start us, length us, event | category | flops | bytes accessed | tf_op | source)
XLA Modules:
  0.0 1251.3 jit_solution(16375797547710604420)
XLA Ops:
  8.7 3.5 collective-permute-start
  16.4 81.7 %all-gather.9.cloned.1.call-done = bf16[1024,544]{1,0:T(8,128)(2,1)} async-done(((bf16[16,544]{1,0:T(8,128)(2,1)}), bf16[1024,544]{1,0:T(8,128)(2,1)}) %all-gather.9.cloned.1.call-update) | async-done | bytes 1114128 | tf_op jit(solution)/shard_map/all_gather | solution.py:108
  101.8 63.4 %all-reduce.15.cloned.1.call-done = f32[128,544]{0,1:T(8,128)} async-done(((f32[128,544]{0,1:T(8,128)}), f32[128,544]{0,1:T(8,128)}) %all-reduce.15.cloned.1.call-update) | async-done | bytes 278544 | tf_op jit(solution)/shard_map/psum | solution.py:112
  167.4 85.5 %all-gather.11.cloned.1.call-done = bf16[512,1024]{1,0:T(8,128)(2,1)} async-done(((bf16[8,1024]{1,0:T(8,128)(2,1)}), bf16[512,1024]{1,0:T(8,128)(2,1)}) %all-gather.11.cloned.1.call-update) | async-done | bytes 1048592 | tf_op jit(solution)/shard_map/all_gather | solution.py:109
  256.4 59.0 %while.128 = (s32[]{:T(128)}, f32[16,1024]{1,0:T(8,128)S(1)}, f32[8,16,1024]{2,1,0:T(8,128)S(1)}, f32[8,16,1024]{2,1,0:T(8,128)S(1)}, f32[8,16,1024]{2,1,0:T(8,1...) while((s32[]{:T(128)}, f32[16,1024]{1,0:T(8,128)S(1)}, ...), condition=%wide.region_6.7_spmd.clone.clone, body=%wide.region_2.6_spmd.clone.clone.sunk | while | flops 26214400 | bytes 9574793 | solution.py:57
  257.6 5.7 multiply_reduce_fusion.25
  265.0 5.7 multiply_reduce_fusion.25
  272.4 5.7 multiply_reduce_fusion.25
  279.8 5.7 multiply_reduce_fusion.25
  287.1 5.7 multiply_reduce_fusion.25
  294.5 5.7 multiply_reduce_fusion.25
  301.9 5.7 multiply_reduce_fusion.25
  309.2 5.7 multiply_reduce_fusion.25
  316.7 83.6 %all-gather.15.cloned.1.call-done = f32[1024,1024]{1,0:T(8,128)} async-done(((f32[16,1024]{1,0:T(8,128)}), f32[1024,1024]{1,0:T(8,128)}) %all-gather.15.cloned.1.call-update) | async-done | bytes 4194320 | tf_op jit(solution)/shard_map/all_gather | solution.py:19
  400.3 87.8 %all-gather.13.cloned.1.call-done = f32[1024,1024]{1,0:T(8,128)} async-done(((f32[16,1024]{1,0:T(8,128)}), f32[1024,1024]{1,0:T(8,128)}) %all-gather.13.cloned.1.call-update) | async-done | bytes 4194320 | tf_op jit(solution)/shard_map/all_gather | solution.py:19
  488.1 59.9 %while.129 = (s32[]{:T(128)}, f32[16,1024]{1,0:T(8,128)S(1)}, s32[]{:T(128)}, f32[64,16,1024]{2,1,0:T(8,128)}, f32[64,16,1024]{2,1,0:T(8,128)}, /*index=5*/s32[]{:T(128)}, s32[]{:T(128)}) while((s32[]{:T(128)}, f32[16,1024]{1,0:T(8,128)S(1)}, s32[]{:T(128)}, f32[64,16,1024]{2,1,0:T(8,128)}, f32[64,16,1024]{2,1,0:T(8,128)}, ...), condition=%wide.region_8.9_spmd.clone, body=%wide.region_7.8_spmd.clone.sunk | while | flops 65540 | bytes 262245 | solution.py:30
  549.1 14.5 %while.126 = (s32[]{:T(128)}, f32[16,1024]{1,0:T(8,128)S(1)}, f32[8,16,1024]{2,1,0:T(8,128)S(1)}, f32[8,16,1024]{2,1,0:T(8,128)}, f32[8,16,1024]{2,1,0:T(8,128)S...) while((s32[]{:T(128)}, f32[16,1024]{1,0:T(8,128)S(1)}, ...), condition=%wide.region_12.13_spmd, body=%wide.region_9.12_spmd.sunk | while | flops 4964354 | bytes 1969769 | solution.py:76
  563.6 8.2 while.127
  573.4 83.1 %all-gather.17.cloned.1.call-done = f32[1024,1024]{1,0:T(8,128)} async-done(((f32[16,1024]{1,0:T(8,128)}), f32[1024,1024]{1,0:T(8,128)}) %all-gather.17.cloned.1.call-update) | async-done | bytes 4194320 | tf_op jit(solution)/shard_map/all_gather | solution.py:19
  656.5 60.4 %while.130 = (s32[]{:T(128)}, f32[16,1024]{1,0:T(8,128)S(1)}, s32[]{:T(128)}, f32[64,16,1024]{2,1,0:T(8,128)}, f32[64,16,1024]{2,1,0:T(8,128)}, /*index=5*/s32[]{:T(128)}, s32[]{:T(128)}, s32[]{:T(128)}, s32[]{:T(128)}) while((s32[]{:T(128)}, f32[16,1024]{1,0:T(8,128)S(1)}, s32[]{:T(128)}, f32[64,16,1024]{2,1,0:T(8,128)}, ...), condition=%wide.region_18.19_spmd.clone, body=%wide.region_17.18_spmd.clone.sunk | while | flops 65544 | bytes 262307 | solution.py:30
  716.9 22.7 %while.132 = (s32[]{:T(128)}, f32[16,1024]{1,0:T(8,128)S(1)}, f32[16,1024]{1,0:T(8,128)S(1)}, f32[8,16,1024]{2,1,0:T(8,128)S(1)}, f32[8,16,16]{2,1,0:T(8,128)S(1...) while((s32[]{:T(128)}, f32[16,1024]{1,0:T(8,128)S(1)}, ...), condition=%wide.region_40.41_spmd.clone, body=%wide.region_33.40_spmd.clone.sunk | while | flops 12041988 | bytes 4084903 | solution.py:76
  742.0 138.3 %while.131 = (s32[]{:T(128)}, f32[16,1024]{1,0:T(8,128)S(1)}, f32[16,1024]{1,0:T(8,128)S(1)}, f32[8,16,1024]{2,1,0:T(8,128)}, f32[8,16,1024]{2,1,0:T(8,128)}, /*...) while((s32[]{:T(128)}, f32[16,1024]{1,0:T(8,128)S(1)}, ...), condition=%wide.region_32.33_spmd.clone, body=%wide.region_19.32_spmd.clone.sunk | while | flops 68452096 | bytes 19686096 | solution.py:57
  745.2 10.7 fusion.106
  762.5 10.7 fusion.106
  779.8 10.7 fusion.106
  797.1 10.7 fusion.106
  814.3 10.7 fusion.106
  831.6 10.7 fusion.106
  848.9 10.7 fusion.106
  866.1 10.7 fusion.106
  892.4 57.6 %all-reduce.17.cloned.1.call-done = bf16[128,544]{1,0:T(8,128)(2,1)} async-done(((bf16[128,544]{1,0:T(8,128)(2,1)}), bf16[128,544]{1,0:T(8,128)(2,1)}) %all-reduce.17.cloned.1.call-update) | async-done | bytes 139280 | tf_op jit(solution)/shard_map/psum | solution.py:158
  958.9 280.4 %all-reduce.9 = (f32[4,1024]{1,0:T(4,128)S(1)}, f32[1024]{0:T(1024)S(1)}, f32[1024]{0:T(1024)S(1)}, f32[1024]{0:T(1024)S(1)}) all-reduce(f32[4,1024]{1,0:T(4,128)S(1)} %pad_maximum_fusion.3, f32[1024]{0:T(1024)S(1)} %get-tuple-element.1399, f32[1024]{0:T(1024)S(1)} %copy-done.25, ...), channel_id=6, replica_groups=mesh['ctx'=64,'mp'=8] {'ctx'}, use_global_device_ids=true, to_apply=%region_47.48.clone | all-reduce | flops 7168 | bytes 57344
  (640 shorter events, 272.3 us)
Async XLA Ops:
  7.2 245.7 %copy-start.26 = (f32[1024]{0:T(1024)S(1)}, f32[1024]{0:T(1024)}, u32[]{:S(2)}) copy-start(f32[1024]{0:T(1024)} %param.33) | copy-start | bytes 12292
  7.2 248.4 %copy-start.12 = (f32[16,1024]{1,0:T(8,128)S(1)}, f32[16,1024]{1,0:T(8,128)}, u32[]{:S(2)}) copy-start(f32[16,1024]{1,0:T(8,128)} %param.34) | copy-start | bytes 196612
  7.2 91.0 %all-gather.9.cloned.1.call-start = ((), (), s32[]{:S(2)}) async-start(), calls=%async_computation | async-start | bytes 1331200 | tf_op jit(solution)/shard_map/all_gather | solution.py:108
  7.9 157.3 %all-reduce.15.cloned.1.call-start = ((), (), s32[]{:S(2)}) async-start(), calls=%async_computation.1 | async-start | bytes 557056 | tf_op jit(solution)/shard_map/psum | solution.py:112
  8.7 5.1 collective-permute-start
  13.1 88.6 %copy-start.14 = (f32[1,1024]{1,0:T(1,128)}, f32[1,1024]{1,0:T(1,128)S(1)}, u32[]{:S(2)}) copy-start(f32[1,1024]{1,0:T(1,128)S(1)} %get-tuple-element.1561) | copy-start | bytes 12292
  13.1 88.6 %copy-start.16 = (f32[1,1024]{1,0:T(1,128)}, f32[1,1024]{1,0:T(1,128)S(1)}, u32[]{:S(2)}) copy-start(f32[1,1024]{1,0:T(1,128)S(1)} %get-tuple-element.1562) | copy-start | bytes 12292
  13.1 88.6 %copy-start.18 = (f32[1,1024]{1,0:T(1,128)}, f32[1,1024]{1,0:T(1,128)S(1)}, u32[]{:S(2)}) copy-start(f32[1,1024]{1,0:T(1,128)S(1)} %get-tuple-element.1563) | copy-start | bytes 12292
  13.1 88.6 %copy-start.20 = (f32[1,1024]{1,0:T(1,128)}, f32[1,1024]{1,0:T(1,128)S(1)}, u32[]{:S(2)}) copy-start(f32[1,1024]{1,0:T(1,128)S(1)} %get-tuple-element.1564) | copy-start | bytes 12292
  13.8 241.8 %copy-start.28 = (f32[128]{0:T(128)}, f32[128]{0:T(128)S(1)}, u32[]{:S(2)}) copy-start(f32[128]{0:T(128)S(1)} %convert_negate_fusion.1) | copy-start | bytes 1540
  13.8 87.9 %copy-start.22 = (bf16[3,1024]{1,0:T(4,128)(2,1)}, bf16[3,1024]{1,0:T(4,128)(2,1)S(1)}, u32[]{:S(2)}) copy-start(bf16[3,1024]{1,0:T(4,128)(2,1)S(1)} %collective-permute-done) | copy-start | bytes 18436
  100.9 152.0 %all-gather.11.cloned.1.call-start = ((), (), s32[]{:S(2)}) async-start(), calls=%async_computation.2 | async-start | bytes 1064960 | tf_op jit(solution)/shard_map/all_gather | solution.py:109
  101.6 298.7 %all-gather.15.cloned.1.call-start = ((), (), s32[]{:S(2)}) async-start(), calls=%async_computation.5 | async-start | bytes 4259840 | tf_op jit(solution)/shard_map/all_gather | solution.py:19
  315.4 232.7 %copy-start.7 = (f32[8,16,1024]{2,1,0:T(8,128)}, f32[8,16,1024]{2,1,0:T(8,128)S(1)}, u32[]{:S(2)}) copy-start(f32[8,16,1024]{2,1,0:T(8,128)S(1)} %get-tuple-element.2193) | copy-start | bytes 1572868
  315.4 232.7 %copy-start.8 = (f32[8,16,1024]{2,1,0:T(8,128)}, f32[8,16,1024]{2,1,0:T(8,128)S(1)}, u32[]{:S(2)}) copy-start(f32[8,16,1024]{2,1,0:T(8,128)S(1)} %get-tuple-element.2194) | copy-start | bytes 1572868
  315.4 232.7 %copy-start.4 = (f32[8,16,1024]{2,1,0:T(8,128)}, f32[8,16,1024]{2,1,0:T(8,128)S(1)}, u32[]{:S(2)}) copy-start(f32[8,16,1024]{2,1,0:T(8,128)S(1)} %get-tuple-element.1049) | copy-start | bytes 1572868
  316.0 172.1 %all-gather.13.cloned.1.call-start = ((), (), s32[]{:S(2)}) async-start(), calls=%async_computation.4 | async-start | bytes 4259840 | tf_op jit(solution)/shard_map/all_gather | solution.py:19
  316.6 339.8 %all-gather.17.cloned.1.call-start = ((), (), s32[]{:S(2)}) async-start(), calls=%async_computation.6 | async-start | bytes 4259840 | tf_op jit(solution)/shard_map/all_gather | solution.py:19
  563.6 153.3 %copy-start.5 = (f32[8,16,1024]{2,1,0:T(8,128)}, f32[8,16,1024]{2,1,0:T(8,128)S(1)}, u32[]{:S(2)}) copy-start(f32[8,16,1024]{2,1,0:T(8,128)S(1)} %get-tuple-element.1050) | copy-start | bytes 1572868
  572.5 377.5 %all-reduce.17.cloned.1.call-start = ((), (), s32[]{:S(2)}) async-start(), calls=%async_computation.3 | async-start | bytes 327680 | tf_op jit(solution)/shard_map/psum | solution.py:158
  742.0 142.3 %copy-start.1 = (bf16[512,1024]{1,0:T(8,128)(2,1)S(1)}, bf16[512,1024]{1,0:T(8,128)(2,1)}, u32[]{:S(2)}) copy-start(bf16[512,1024]{1,0:T(8,128)(2,1)} %all-gather.11.cloned.1.call-done) | copy-start | bytes 3145732
  886.4 63.6 %copy-start.9 = (bf16[1024,544]{1,0:T(8,128)(2,1)S(1)}, bf16[1024,544]{1,0:T(8,128)(2,1)}, u32[]{:S(2)}) copy-start(bf16[1024,544]{1,0:T(8,128)(2,1)} %all-gather.9.cloned.1.call-done) | copy-start | bytes 3342340
  886.4 63.6 %copy-start.10 = (bf16[128,1024]{1,0:T(8,128)(2,1)S(1)}, bf16[128,1024]{1,0:T(8,128)(2,1)}, u32[]{:S(2)}) copy-start(bf16[128,1024]{1,0:T(8,128)(2,1)} %param.25) | copy-start | bytes 786436
  886.4 355.2 %all-reduce.19.cloned.1.call-start = ((), (), s32[]{:S(2)}) async-start(), calls=%async_computation.7 | async-start | bytes 4325376
  888.2 61.8 %copy-start.17 = (f32[1,1024]{1,0:T(1,128)S(1)}, f32[1,1024]{1,0:T(1,128)}, u32[]{:S(2)}) copy-start(f32[1,1024]{1,0:T(1,128)} %copy-done.16) | copy-start | bytes 12292
  888.2 61.8 %copy-start.19 = (f32[1,1024]{1,0:T(1,128)S(1)}, f32[1,1024]{1,0:T(1,128)}, u32[]{:S(2)}) copy-start(f32[1,1024]{1,0:T(1,128)} %copy-done.18) | copy-start | bytes 12292
  888.2 61.8 %copy-start.21 = (f32[1,1024]{1,0:T(1,128)S(1)}, f32[1,1024]{1,0:T(1,128)}, u32[]{:S(2)}) copy-start(f32[1,1024]{1,0:T(1,128)} %copy-done.20) | copy-start | bytes 12292
  888.2 61.8 %copy-start.23 = (bf16[3,1024]{1,0:T(4,128)(2,1)S(1)}, bf16[3,1024]{1,0:T(4,128)(2,1)}, u32[]{:S(2)}) copy-start(bf16[3,1024]{1,0:T(4,128)(2,1)} %copy-done.22) | copy-start | bytes 18436
  888.3 61.8 %copy-start.27 = (f32[1024]{0:T(1024)S(1)}, f32[1024]{0:T(1024)}, u32[]{:S(2)}) copy-start(f32[1024]{0:T(1024)} %param.30) | copy-start | bytes 12292
  892.4 66.5 %copy-start.24 = (f32[1024]{0:T(1024)S(1)}, f32[1024]{0:T(1024)}, u32[]{:S(2)}) copy-start(f32[1024]{0:T(1024)} %get-tuple-element.1526) | copy-start | bytes 12292
  892.4 66.5 %copy-start.25 = (f32[1024]{0:T(1024)S(1)}, f32[1024]{0:T(1024)}, u32[]{:S(2)}) copy-start(f32[1024]{0:T(1024)} %get-tuple-element.1529) | copy-start | bytes 12292
  952.0 5.6 collective-permute-start.1
  (7 other events, 82.2 us)
Sparse Core Ops, SparseCore 0:
  11.1 87.0 all-gather.8
  101.0 64.1 all-reduce.14
  168.7 84.1 all-gather.10
  316.2 84.1 all-gather.14
  404.3 83.8 all-gather.12
  572.6 83.8 all-gather.16
  886.5 63.4 all-reduce.16
  953.5 165.4 all-reduce.18
where the time goes:
time: 1260 us; the launch traced here: 1250 us
  waiting for transfers between devices  547 us (43%)
  other arithmetic  308 us (24%)
  blocking collectives  280 us (22%)
  local copies, waits for them, and re-layouts  80.2 us (6%)
  between operations  16 us (1%)
    unnamed x1, blocking collectives  280 us
    all_gather x3, waiting for transfers between devices, prefix(): everything = jax.tree.map(lambda part: lax.all_gather(part, axis), x)  255 us
    select_n x128, other arithmetic, step(): return jax.tree.map(lambda a, b: jnp.where(reached, a, b), new, before)  117 us
    all_gather x1, waiting for transfers between devices, body(): lax.all_gather(dt_weight, 'ctx', axis=0, tiled=True)  85.5 us
    reduce_sum x8, other arithmetic, block_closed(): gaps = jnp.where(lower, cumul[:, None] - cumul[None, :], 0.0)  85.3 us
    all_gather x1, waiting for transfers between devices, body(): lax.all_gather(proj_weight, 'ctx', axis=0, tiled=True)  81.7 us
    psum x1, waiting for transfers between devices, body(): projected = lax.psum(partial_proj, 'mp')  63.4 us
    psum x1, waiting for transfers between devices, body(): lax.psum(jnp.concatenate([grad_low, grad_bmat, grad_cmat], axis=1).astype...  57.6 us
  transfers between devices with their start and end apart: 10, of which 8 were waited for; matrix products, arithmetic and copies ran while one was open for 2% of the time, Pallas kernels for 0%

commit v1 on v0

--- a/solution.py
+++ b/solution.py
@@ -155,9 +155,9 @@
     grad_low = lax.dot_general(
         grad_pre_half, rows_dt, (((1,), (1,)), ((), ())), preferred_element_type=jnp.float32
     )
-    grad_proj = lax.psum(
-        jnp.concatenate([grad_low, grad_bmat, grad_cmat], axis=1).astype(jnp.bfloat16), "mp"
-    )
+    own = jnp.concatenate([grad_low, grad_bmat, grad_cmat], axis=1).astype(jnp.bfloat16)
+    shards = lax.all_gather(own, "mp")
+    grad_proj = jnp.sum(shards, axis=0)
     grad_from_proj = lax.dot_general(
         grad_proj, rows_proj, (((1,), (1,)), ((), ())), preferred_element_type=jnp.float32
     )

time: 1260 us -> 1220 us (0.968)
  waiting for transfers between devices: 547 us -> 508 us
    psum x1 -> x0, waiting for transfers between devices: 57.6 us -> none  [body(): lax.psum(jnp.concatenate([grad_low, grad_bmat, grad_cmat], axis=1).astype...]
    all_gather x0 -> x1, waiting for transfers between devices: none -> 19.3 us  [body(): shards = lax.all_gather(own, 'mp')]
where the time goes in v1:
time: 1220 us; the launch traced here: 1210 us
  waiting for transfers between devices  508 us (42%)
  other arithmetic  306 us (25%)
  blocking collectives  281 us (23%)
  local copies, waits for them, and re-layouts  75.5 us (6%)
  between operations  16.1 us (1%)
    unnamed x1, blocking collectives  281 us
    all_gather x3, waiting for transfers between devices, prefix(): everything = jax.tree.map(lambda part: lax.all_gather(part, axis), x)  255 us
    select_n x128, other arithmetic, step(): return jax.tree.map(lambda a, b: jnp.where(reached, a, b), new, before)  117 us
    all_gather x1, waiting for transfers between devices, body(): lax.all_gather(dt_weight, 'ctx', axis=0, tiled=True)  85.5 us
    reduce_sum x8, other arithmetic, block_closed(): gaps = jnp.where(lower, cumul[:, None] - cumul[None, :], 0.0)  85.3 us
    all_gather x1, waiting for transfers between devices, body(): lax.all_gather(proj_weight, 'ctx', axis=0, tiled=True)  81.7 us
    psum x1, waiting for transfers between devices, body(): projected = lax.psum(partial_proj, 'mp')  63.4 us
    reduce_sum x8, other arithmetic, block_closed(): jnp.sum(weights * inflow[None], axis=1)  45.4 us
  transfers between devices with their start and end apart: 10, of which 8 were waited for; matrix products, arithmetic and copies ran while one was open for 2% of the time, Pallas kernels for 0%

profile of v1, /device:TPU:6, one launch (start us, length us, event | category | flops | bytes accessed | tf_op | source)
XLA Modules:
  0.0 1206.9 jit_solution(17664871756566632417)
XLA Ops:
  8.7 3.5 collective-permute-start
  16.4 81.7 %all-gather.10.cloned.1.call-done = bf16[1024,544]{1,0:T(8,128)(2,1)} async-done(((bf16[16,544]{1,0:T(8,128)(2,1)}), bf16[1024,544]{1,0:T(8,128)(2,1)}) %all-gather.10.cloned.1.call-update) | async-done | bytes 1114128 | tf_op jit(solution)/shard_map/all_gather | solution.py:108
  101.8 63.4 %all-reduce.14.cloned.1.call-done = f32[128,544]{0,1:T(8,128)} async-done(((f32[128,544]{0,1:T(8,128)}), f32[128,544]{0,1:T(8,128)}) %all-reduce.14.cloned.1.call-update) | async-done | bytes 278544 | tf_op jit(solution)/shard_map/psum | solution.py:112
  167.4 85.5 %all-gather.12.cloned.1.call-done = bf16[512,1024]{1,0:T(8,128)(2,1)} async-done(((bf16[8,1024]{1,0:T(8,128)(2,1)}), bf16[512,1024]{1,0:T(8,128)(2,1)}) %all-gather.12.cloned.1.call-update) | async-done | bytes 1048592 | tf_op jit(solution)/shard_map/all_gather | solution.py:109
  256.4 59.0 %while.128 = (s32[]{:T(128)}, f32[16,1024]{1,0:T(8,128)S(1)}, f32[8,16,1024]{2,1,0:T(8,128)S(1)}, f32[8,16,1024]{2,1,0:T(8,128)S(1)}, f32[8,16,1024]{2,1,0:T(8,1...) while((s32[]{:T(128)}, f32[16,1024]{1,0:T(8,128)S(1)}, ...), condition=%wide.region_6.7_spmd.clone.clone, body=%wide.region_2.6_spmd.clone.clone.sunk | while | flops 26214400 | bytes 9574793 | solution.py:57
  257.6 5.7 multiply_reduce_fusion.25
  265.0 5.7 multiply_reduce_fusion.25
  272.4 5.7 multiply_reduce_fusion.25
  279.8 5.7 multiply_reduce_fusion.25
  287.1 5.7 multiply_reduce_fusion.25
  294.5 5.7 multiply_reduce_fusion.25
  301.9 5.7 multiply_reduce_fusion.25
  309.2 5.7 multiply_reduce_fusion.25
  316.7 83.6 %all-gather.18.cloned.1.call-done = f32[1024,1024]{1,0:T(8,128)} async-done(((f32[16,1024]{1,0:T(8,128)}), f32[1024,1024]{1,0:T(8,128)}) %all-gather.18.cloned.1.call-update) | async-done | bytes 4194320 | tf_op jit(solution)/shard_map/all_gather | solution.py:19
  400.3 87.8 %all-gather.16.cloned.1.call-done = f32[1024,1024]{1,0:T(8,128)} async-done(((f32[16,1024]{1,0:T(8,128)}), f32[1024,1024]{1,0:T(8,128)}) %all-gather.16.cloned.1.call-update) | async-done | bytes 4194320 | tf_op jit(solution)/shard_map/all_gather | solution.py:19
  488.1 59.9 %while.129 = (s32[]{:T(128)}, f32[16,1024]{1,0:T(8,128)S(1)}, s32[]{:T(128)}, f32[64,16,1024]{2,1,0:T(8,128)}, f32[64,16,1024]{2,1,0:T(8,128)}, /*index=5*/s32[]{:T(128)}, s32[]{:T(128)}) while((s32[]{:T(128)}, f32[16,1024]{1,0:T(8,128)S(1)}, s32[]{:T(128)}, f32[64,16,1024]{2,1,0:T(8,128)}, f32[64,16,1024]{2,1,0:T(8,128)}, ...), condition=%wide.region_8.9_spmd.clone, body=%wide.region_7.8_spmd.clone.sunk | while | flops 65540 | bytes 262245 | solution.py:30
  549.1 14.5 %while.126 = (s32[]{:T(128)}, f32[16,1024]{1,0:T(8,128)S(1)}, f32[8,16,1024]{2,1,0:T(8,128)S(1)}, f32[8,16,1024]{2,1,0:T(8,128)}, f32[8,16,1024]{2,1,0:T(8,128)S...) while((s32[]{:T(128)}, f32[16,1024]{1,0:T(8,128)S(1)}, ...), condition=%wide.region_12.13_spmd, body=%wide.region_9.12_spmd.sunk | while | flops 4964354 | bytes 1969769 | solution.py:76
  563.6 8.2 while.127
  573.4 83.1 %all-gather.20.cloned.1.call-done = f32[1024,1024]{1,0:T(8,128)} async-done(((f32[16,1024]{1,0:T(8,128)}), f32[1024,1024]{1,0:T(8,128)}) %all-gather.20.cloned.1.call-update) | async-done | bytes 4194320 | tf_op jit(solution)/shard_map/all_gather | solution.py:19
  656.5 60.4 %while.130 = (s32[]{:T(128)}, f32[16,1024]{1,0:T(8,128)S(1)}, s32[]{:T(128)}, f32[64,16,1024]{2,1,0:T(8,128)}, f32[64,16,1024]{2,1,0:T(8,128)}, /*index=5*/s32[]{:T(128)}, s32[]{:T(128)}, s32[]{:T(128)}, s32[]{:T(128)}) while((s32[]{:T(128)}, f32[16,1024]{1,0:T(8,128)S(1)}, s32[]{:T(128)}, f32[64,16,1024]{2,1,0:T(8,128)}, ...), condition=%wide.region_18.19_spmd.clone, body=%wide.region_17.18_spmd.clone.sunk | while | flops 65544 | bytes 262307 | solution.py:30
  716.9 22.7 %while.132 = (s32[]{:T(128)}, f32[16,1024]{1,0:T(8,128)S(1)}, f32[16,1024]{1,0:T(8,128)S(1)}, f32[8,16,1024]{2,1,0:T(8,128)S(1)}, f32[8,16,16]{2,1,0:T(8,128)S(1...) while((s32[]{:T(128)}, f32[16,1024]{1,0:T(8,128)S(1)}, ...), condition=%wide.region_40.41_spmd.clone, body=%wide.region_33.40_spmd.clone.sunk | while | flops 12041988 | bytes 4084903 | solution.py:76
  741.4 133.5 %while.131 = (s32[]{:T(128)}, f32[16,1024]{1,0:T(8,128)S(1)}, f32[16,1024]{1,0:T(8,128)S(1)}, f32[8,16,1024]{2,1,0:T(8,128)}, f32[8,16,1024]{2,1,0:T(8,128)}, /*...) while((s32[]{:T(128)}, f32[16,1024]{1,0:T(8,128)S(1)}, ...), condition=%wide.region_32.33_spmd.clone, body=%wide.region_19.32_spmd.clone.sunk | while | flops 68452096 | bytes 19693264 | solution.py:57
  744.6 10.7 fusion.107
  761.3 10.7 fusion.107
  778.0 10.7 fusion.107
  794.7 10.7 fusion.107
  811.4 10.7 fusion.107
  828.0 10.7 fusion.107
  844.7 10.7 fusion.107
  861.4 10.7 fusion.107
  884.8 19.3 %all-gather.14.cloned.1.call-done = bf16[8,128,544]{1,2,0:T(8,128)(2,1)} async-done(((bf16[1,128,544]{1,2,0:T(8,128)(2,1)}), bf16[8,128,544]{1,2,0:T(8,128)(2,1)}) %all-gather.14.cloned.1.call-update) | async-done | bytes 1114128 | tf_op jit(solution)/shard_map/all_gather | solution.py:159
  914.3 280.6 %all-reduce.9 = (f32[4,1024]{1,0:T(4,128)S(1)}, f32[1024]{0:T(1024)S(1)}, f32[1024]{0:T(1024)S(1)}, f32[1024]{0:T(1024)S(1)}) all-reduce(f32[4,1024]{1,0:T(4,128)S(1)} %pad_maximum_fusion.3, f32[1024]{0:T(1024)S(1)} %get-tuple-element.1448, f32[1024]{0:T(1024)S(1)} %copy-done.27, ...), channel_id=6, replica_groups=mesh['ctx'=64,'mp'=8] {'ctx'}, use_global_device_ids=true, to_apply=%region_47.48.clone | all-reduce | flops 7168 | bytes 57344
  (646 shorter events, 265.9 us)
Async XLA Ops:
  7.2 245.7 %copy-start.28 = (f32[1024]{0:T(1024)S(1)}, f32[1024]{0:T(1024)}, u32[]{:S(2)}) copy-start(f32[1024]{0:T(1024)} %param.33) | copy-start | bytes 12292
  7.2 248.4 %copy-start.13 = (f32[16,1024]{1,0:T(8,128)S(1)}, f32[16,1024]{1,0:T(8,128)}, u32[]{:S(2)}) copy-start(f32[16,1024]{1,0:T(8,128)} %param.34) | copy-start | bytes 196612
  7.2 91.0 %all-gather.10.cloned.1.call-start = ((), (), s32[]{:S(2)}) async-start(), calls=%async_computation | async-start | bytes 1331200 | tf_op jit(solution)/shard_map/all_gather | solution.py:108
  7.9 157.3 %all-reduce.14.cloned.1.call-start = ((), (), s32[]{:S(2)}) async-start(), calls=%async_computation.1 | async-start | bytes 557056 | tf_op jit(solution)/shard_map/psum | solution.py:112
  8.7 5.1 collective-permute-start
  13.1 88.6 %copy-start.16 = (f32[1,1024]{1,0:T(1,128)}, f32[1,1024]{1,0:T(1,128)S(1)}, u32[]{:S(2)}) copy-start(f32[1,1024]{1,0:T(1,128)S(1)} %get-tuple-element.1610) | copy-start | bytes 12292
  13.1 88.6 %copy-start.18 = (f32[1,1024]{1,0:T(1,128)}, f32[1,1024]{1,0:T(1,128)S(1)}, u32[]{:S(2)}) copy-start(f32[1,1024]{1,0:T(1,128)S(1)} %get-tuple-element.1611) | copy-start | bytes 12292
  13.1 88.6 %copy-start.20 = (f32[1,1024]{1,0:T(1,128)}, f32[1,1024]{1,0:T(1,128)S(1)}, u32[]{:S(2)}) copy-start(f32[1,1024]{1,0:T(1,128)S(1)} %get-tuple-element.1612) | copy-start | bytes 12292
  13.1 88.6 %copy-start.22 = (f32[1,1024]{1,0:T(1,128)}, f32[1,1024]{1,0:T(1,128)S(1)}, u32[]{:S(2)}) copy-start(f32[1,1024]{1,0:T(1,128)S(1)} %get-tuple-element.1613) | copy-start | bytes 12292
  13.8 241.8 %copy-start.30 = (f32[128]{0:T(128)}, f32[128]{0:T(128)S(1)}, u32[]{:S(2)}) copy-start(f32[128]{0:T(128)S(1)} %convert_negate_fusion.1) | copy-start | bytes 1540
  13.8 87.9 %copy-start.24 = (bf16[3,1024]{1,0:T(4,128)(2,1)}, bf16[3,1024]{1,0:T(4,128)(2,1)S(1)}, u32[]{:S(2)}) copy-start(bf16[3,1024]{1,0:T(4,128)(2,1)S(1)} %collective-permute-done) | copy-start | bytes 18436
  100.9 152.0 %all-gather.12.cloned.1.call-start = ((), (), s32[]{:S(2)}) async-start(), calls=%async_computation.2 | async-start | bytes 1064960 | tf_op jit(solution)/shard_map/all_gather | solution.py:109
  101.6 298.7 %all-gather.18.cloned.1.call-start = ((), (), s32[]{:S(2)}) async-start(), calls=%async_computation.5 | async-start | bytes 4259840 | tf_op jit(solution)/shard_map/all_gather | solution.py:19
  315.4 232.7 %copy-start.7 = (f32[8,16,1024]{2,1,0:T(8,128)}, f32[8,16,1024]{2,1,0:T(8,128)S(1)}, u32[]{:S(2)}) copy-start(f32[8,16,1024]{2,1,0:T(8,128)S(1)} %get-tuple-element.2242) | copy-start | bytes 1572868
  315.4 232.7 %copy-start.8 = (f32[8,16,1024]{2,1,0:T(8,128)}, f32[8,16,1024]{2,1,0:T(8,128)S(1)}, u32[]{:S(2)}) copy-start(f32[8,16,1024]{2,1,0:T(8,128)S(1)} %get-tuple-element.2243) | copy-start | bytes 1572868
  315.4 232.7 %copy-start.4 = (f32[8,16,1024]{2,1,0:T(8,128)}, f32[8,16,1024]{2,1,0:T(8,128)S(1)}, u32[]{:S(2)}) copy-start(f32[8,16,1024]{2,1,0:T(8,128)S(1)} %get-tuple-element.1049) | copy-start | bytes 1572868
  316.0 172.1 %all-gather.16.cloned.1.call-start = ((), (), s32[]{:S(2)}) async-start(), calls=%async_computation.4 | async-start | bytes 4259840 | tf_op jit(solution)/shard_map/all_gather | solution.py:19
  316.6 339.8 %all-gather.20.cloned.1.call-start = ((), (), s32[]{:S(2)}) async-start(), calls=%async_computation.6 | async-start | bytes 4259840 | tf_op jit(solution)/shard_map/all_gather | solution.py:19
  563.6 153.3 %copy-start.5 = (f32[8,16,1024]{2,1,0:T(8,128)}, f32[8,16,1024]{2,1,0:T(8,128)S(1)}, u32[]{:S(2)}) copy-start(f32[8,16,1024]{2,1,0:T(8,128)S(1)} %get-tuple-element.1050) | copy-start | bytes 1572868
  572.5 331.6 %all-gather.14.cloned.1.call-start = ((), (), s32[]{:S(2)}) async-start(), calls=%async_computation.3 | async-start | bytes 1253376 | tf_op jit(solution)/shard_map/all_gather | solution.py:159
  741.4 136.8 %copy-start.1 = (bf16[512,1024]{1,0:T(8,128)(2,1)S(1)}, bf16[512,1024]{1,0:T(8,128)(2,1)}, u32[]{:S(2)}) copy-start(bf16[512,1024]{1,0:T(8,128)(2,1)} %all-gather.12.cloned.1.call-done) | copy-start | bytes 3145732
  879.6 317.7 %all-reduce.16.cloned.1.call-start = ((), (), s32[]{:S(2)}) async-start(), calls=%async_computation.7 | async-start | bytes 4325376
  882.1 23.5 %copy-start.9 = (bf16[1024,544]{1,0:T(8,128)(2,1)S(1)}, bf16[1024,544]{1,0:T(8,128)(2,1)}, u32[]{:S(2)}) copy-start(bf16[1024,544]{1,0:T(8,128)(2,1)} %all-gather.10.cloned.1.call-done) | copy-start | bytes 3342340
  882.1 23.5 %copy-start.10 = (bf16[128,1024]{1,0:T(8,128)(2,1)S(1)}, bf16[128,1024]{1,0:T(8,128)(2,1)}, u32[]{:S(2)}) copy-start(bf16[128,1024]{1,0:T(8,128)(2,1)} %param.25) | copy-start | bytes 786436
  882.1 23.5 %copy-start.17 = (f32[1,1024]{1,0:T(1,128)S(1)}, f32[1,1024]{1,0:T(1,128)}, u32[]{:S(2)}) copy-start(f32[1,1024]{1,0:T(1,128)} %copy-done.16) | copy-start | bytes 12292
  882.1 23.5 %copy-start.19 = (f32[1,1024]{1,0:T(1,128)S(1)}, f32[1,1024]{1,0:T(1,128)}, u32[]{:S(2)}) copy-start(f32[1,1024]{1,0:T(1,128)} %copy-done.18) | copy-start | bytes 12292
  882.1 23.5 %copy-start.21 = (f32[1,1024]{1,0:T(1,128)S(1)}, f32[1,1024]{1,0:T(1,128)}, u32[]{:S(2)}) copy-start(f32[1,1024]{1,0:T(1,128)} %copy-done.20) | copy-start | bytes 12292
  882.1 23.5 %copy-start.23 = (f32[1,1024]{1,0:T(1,128)S(1)}, f32[1,1024]{1,0:T(1,128)}, u32[]{:S(2)}) copy-start(f32[1,1024]{1,0:T(1,128)} %copy-done.22) | copy-start | bytes 12292
  882.1 23.5 %copy-start.25 = (bf16[3,1024]{1,0:T(4,128)(2,1)S(1)}, bf16[3,1024]{1,0:T(4,128)(2,1)}, u32[]{:S(2)}) copy-start(bf16[3,1024]{1,0:T(4,128)(2,1)} %copy-done.24) | copy-start | bytes 18436
  882.1 23.5 %copy-start.29 = (f32[1024]{0:T(1024)S(1)}, f32[1024]{0:T(1024)}, u32[]{:S(2)}) copy-start(f32[1024]{0:T(1024)} %param.30) | copy-start | bytes 12292
  905.5 8.8 copy-start.26
  907.4 5.6 collective-permute-start.1
  (9 other events, 37.2 us)
Sparse Core Ops, SparseCore 0:
  11.1 87.0 all-gather.9
  101.0 64.1 all-reduce.13
  168.7 84.1 all-gather.11
  316.2 84.1 all-gather.17
  404.3 83.8 all-gather.15
  572.6 83.8 all-gather.19
  879.8 24.2 all-gather.13
  907.9 164.9 all-reduce.15
